TPU v7x, 512 devices: a whole 4x4x16 slice. The times are simulated.
512 devices in a mesh: chan: 32 (over y, z_lo, core), freq: 16 (over z_hi, x).
Axes of the slice: x: 4, y: 4, z: 16 (z_hi: 4, z_lo: 4; z = z_hi * 4 + z_lo), core: 2. Of those that a mesh axis runs over, the one named last changes fastest.
Arguments:
- spectra: bfloat16 [2, 30, 1024, 4096], P(None, None, 'freq', 'chan'), may hold values from -6 to 6
- src_ids: int32 [2, 32], replicated, may hold values from 0 to 4095
- pair_bin: int32 [2, 32, 4096], P(None, None, 'chan'), may hold values from 0 to 1023, as said below
- slot_of_bin: int32 [1024], replicated, may hold values from 0 to 1023, each once
Outputs:
- offset_gather: float32 [1024, 256], P('chan')
Inputs may be any that keep to these rules, and one draw needn't show every extreme that they name: slot_of_bin names every row of offset_gather once. `pair_bin`: some offset bins are named by no pair.
All inputs are finite; a program needn't handle non-finite values.
Results may differ from a plain program's by a relative error of at most 0.0003.
Values may be sent and summed in bfloat16 or wider, within the bound.
A program may use at most 64 MiB of HBM per device.

v0:
```python
import math

import jax
import jax.numpy as jnp
from jax import lax
from jax.sharding import PartitionSpec as P

F = 1024
NLAG = 256


def lag_basis(anchor, amount, totals, lag_count, windows):
    frequency = anchor + lax.iota(jnp.int32, amount)
    shifts = lax.iota(jnp.int32, lag_count) - lag_count // 2
    phases = frequency[:, None] * shifts[None, :] % (2 * totals)
    angles = phases.astype(jnp.float32) * (math.pi / totals)
    factor = 1.0 / math.sqrt(windows * totals)
    return jnp.concatenate([jnp.cos(angles), -jnp.sin(angles)], axis=0) * factor


def picked(spectra, wanted):
    chans = spectra.shape[3]
    chan_ids = lax.axis_index("chan") * chans + lax.iota(jnp.int32, chans)
    picker = (chan_ids[:, None] == wanted[None, :]).astype(spectra.dtype)
    return jnp.einsum("kwfc,cs->kwfs", spectra, picker, preferred_element_type=jnp.float32)


def cross_terms(source, spectra):
    flipped = jnp.stack([-source[1], source[0]])
    stacked = jnp.stack([source, flipped])
    crossed = jnp.einsum("jkwfs,kwfc->scjf", stacked, spectra, preferred_element_type=jnp.float32)
    return crossed.reshape(source.shape[3] * spectra.shape[3], 2 * spectra.shape[2])


def body(spectra, src_ids, pair_bin, slot_of_bin):
    windows = spectra.shape[1]
    freq_dev = spectra.shape[2]
    steps = pair_bin.shape[0]
    bin_total = slot_of_bin.shape[0]
    lag_table = lag_basis(lax.axis_index("freq") * freq_dev, freq_dev, F, NLAG, windows)
    counts = jnp.zeros((bin_total,), jnp.float32)
    summed = jnp.zeros((bin_total, NLAG), jnp.float32)
    for step_no in range(steps):
        source = lax.psum(picked(spectra, src_ids[step_no]).astype(jnp.bfloat16), "chan")
        crossed = cross_terms(source, spectra)
        bin_ids = pair_bin[step_no].reshape(-1)
        counts = counts + jax.ops.segment_sum(
            jnp.ones((bin_ids.shape[0],), jnp.float32), bin_ids, num_segments=bin_total
        )
        traces = jnp.dot(crossed, lag_table, precision=lax.Precision.HIGHEST)
        summed = summed + jax.ops.segment_sum(traces, bin_ids, num_segments=bin_total)
    summed = jax.ops.segment_sum(summed, slot_of_bin, num_segments=bin_total)
    counts = jax.ops.segment_sum(counts, slot_of_bin, num_segments=bin_total)
    owned, owned_counts = (
        lax.psum_scatter(summed, "chan", scatter_dimension=0, tiled=True),
        lax.psum_scatter(counts, "chan", scatter_dimension=0, tiled=True),
    )
    totals = lax.psum(owned, "freq")
    return totals / jnp.sqrt(jnp.maximum(owned_counts, 1.0))[:, None]


def solution(mesh):
    return jax.shard_map(
        body,
        mesh=mesh,
        in_specs=(P(None, None, "freq", "chan"), P(), P(None, None, "chan"), P()),
        out_specs=P("chan", None),
        check_vma=False,
    )
```

profile of v0, /device:TPU:128, one launch (start us, length us, event | category | flops | bytes accessed | tf_op | source)
XLA Modules:
  0.0 636.5 jit_solution(4346508088757996681)
XLA Ops:
  6.5 0.0 copy-start
  6.5 0.0 copy-start.4
  6.5 0.0 all-reduce.4.cloned.1.call-start
  6.5 0.8 slice_bitcast_fusion.2
  7.3 0.4 copy-done
  7.8 1.8 fusion.6
  9.6 1.8 fusion.7
  11.4 0.0 all-reduce.4.cloned.1.call-update
  11.4 0.0 reduce-scatter.2.cloned.1.call-start
  11.5 0.0 copy-done.4
  11.5 0.3 fusion.22
  11.9 288.8 %all-reduce.4.cloned.1.call-done = (bf16[2,30,64,32]{2,3,1,0:T(8,128)(2,1)}, bf16[2,30,64,32]{2,3,1,0:T(8,128)(2,1)}) async-done(((bf16[2,30,64,32]{2,3,1,0:T(8,128)(2,1)}, bf16[2,30,64,32]{2,3,1,0:T(8,128)(2,1)}), (bf16[2,30,64,32]{2,3,1,0:T(8,128)(2,1)}, bf16[2,30,64,32]{2,3,1,0:T(8,128)(2,1)})) %all-reduce.4.cloned.1.call-update) | async-done | bytes 491536 | tf_op jit(solution)/shard_map/psum | solution.py:44
  300.6 0.0 copy-start.2
  300.6 2.1 slice_negate_fusion
  302.8 0.1 maximum_bitcast_fusion
  302.9 0.0 copy-done.2
  302.9 1.2 pad_maximum_fusion
  304.1 4.5 copy.15
  308.6 1.2 convolution_bitcast_fusion.1
  309.7 0.0 copy-start.3
  309.7 0.0 copy-start.1
  309.7 0.2 copy.17
  309.9 0.7 copy-done.3
  310.7 0.1 maximum_bitcast_fusion.1
  310.8 0.1 copy-done.1
  310.9 1.2 pad_maximum_fusion.1
  312.1 5.3 copy.18
  317.4 2.8 convolution_bitcast_fusion
  320.2 0.2 copy.20
  320.4 6.1 fusion.3
  326.5 6.1 fusion
  332.6 23.3 %scatter_custom_fusion = f32[1024,256]{1,0:T(8,128)S(1)} fusion(s32[4096]{0:T(1024)S(1)} %get-tuple-element.12, f32[4096,256]{1,0:T(8,128)} %fusion.3, f32[]{:T(128)} %constant.13.clone.1), kind=kCustom, calls=%fused_computation.27 | custom fusion | flops 1048576 | bytes 1049088 | tf_op jit(solution)/shard_map/scatter-add | solution.py:51
  355.9 23.1 %scatter_custom_fusion.1 = f32[1024,256]{1,0:T(8,128)S(1)} fusion(s32[4096]{0:T(1024)S(1)} %get-tuple-element.11, f32[4096,256]{1,0:T(8,128)} %fusion, f32[]{:T(128)} %constant.13.clone.1), kind=kCustom, calls=%fused_computation.25 | custom fusion | flops 1048576 | bytes 1049088 | tf_op jit(solution)/shard_map/scatter-add | solution.py:51
  379.0 7.3 %scatter_custom_fusion.2 = f32[1024,256]{1,0:T(8,128)} fusion(s32[1024]{0:T(1024)} %param.7, f32[1024,256]{1,0:T(8,128)S(1)} %scatter_custom_fusion, f32[1024,256]{1,0:T(8,128)S(1)} %scatter_custom_fusion.1, f32[]{:T(128)} %constant.13.clone.1), kind=kCustom, calls=%fused_computation.18 | custom fusion | flops 524288 | bytes 3146240 | tf_op jit(solution)/shard_map/scatter-add | solution.py:52
  386.3 0.0 reduce-scatter.2.cloned.1.call-update
  386.3 28.8 %scatter_custom_fusion.3 = f32[1024]{0:T(1024)S(1)} fusion(s32[4096]{0:T(1024)S(1)} %get-tuple-element.12, f32[4096]{0:T(1024)S(1)} %broadcast.36, f32[]{:T(128)} %constant.13.clone.1), kind=kCustom, calls=%fused_computation.61 | custom fusion | flops 4096 | bytes 4100 | tf_op jit(solution)/shard_map/scatter-add | solution.py:47
  415.1 28.8 %scatter_custom_fusion.4 = f32[1024]{0:T(1024)S(1)} fusion(s32[4096]{0:T(1024)S(1)} %get-tuple-element.11, f32[4096]{0:T(1024)S(1)} %broadcast.36, f32[]{:T(128)} %constant.13.clone.1), kind=kCustom, calls=%fused_computation.59 | custom fusion | flops 4096 | bytes 4100 | tf_op jit(solution)/shard_map/scatter-add | solution.py:47
  443.9 7.8 %scatter_custom_fusion.5 = f32[1024]{0:T(1024)S(1)} fusion(s32[1024]{0:T(1024)} %param.7, f32[1024]{0:T(1024)S(1)} %add.67, f32[]{:T(128)} %constant.13.clone.1), kind=kCustom, calls=%fused_computation.57 | custom fusion | flops 1024 | bytes 4608 | tf_op jit(solution)/shard_map/scatter-add | solution.py:53
  451.7 1.3 dynamic-slice
  453.6 69.6 %all-reduce = f32[1024]{0:T(1024)S(1)} all-reduce(f32[1024]{0:T(1024)S(1)} %scatter_custom_fusion.5), channel_id=3, replica_groups=mesh['chan'=32,'freq'=16] {'chan'}, use_global_device_ids=true, to_apply=%region_10.11.clone | all-reduce | flops 1024 | bytes 8192
  523.2 0.1 fusion.37
  523.2 12.4 %reduce-scatter.2.cloned.1.call-done = f32[32,256]{1,0:T(8,128)} async-done(((f32[1024,256]{1,0:T(8,128)}), f32[32,256]{1,0:T(8,128)}) %reduce-scatter.2.cloned.1.call-update) | async-done | bytes 32784 | tf_op jit(solution)/shard_map/reduce_scatter | solution.py:55
  535.6 93.4 %psum.23 = f32[32,256]{1,0:T(8,128)S(1)} all-reduce(f32[32,256]{1,0:T(8,128)} %reduce-scatter.2.cloned.1.call-done), channel_id=1, replica_groups=mesh['chan'=32,'freq'=16] {'freq'}, use_global_device_ids=true, to_apply=%region_6.7 | all-reduce | flops 8192 | bytes 65536 | tf_op jit(solution)/shard_map/psum | solution.py:58
  629.0 0.7 broadcast_divide_fusion
  (6 shorter events, 0.0 us)
Async XLA Ops:
  6.5 1.2 copy-start
  6.5 5.0 copy-start.4
  6.5 294.1 %all-reduce.4.cloned.1.call-start = ((), (), s32[]{:S(2)}) async-start(), calls=%async_computation.2 | async-start | bytes 1966080 | tf_op jit(solution)/shard_map/psum | solution.py:44
  11.4 524.2 %reduce-scatter.2.cloned.1.call-start = ((), (), s32[]{:S(2)}) async-start(), calls=%async_computation.1 | async-start | bytes 1081344 | tf_op jit(solution)/shard_map/reduce_scatter | solution.py:55
  300.6 2.3 copy-start.2
  309.7 0.9 copy-start.3
  309.7 1.2 copy-start.1
Sparse Core Ops, SparseCore 0:
  11.6 289.0 all-reduce.3
  386.4 149.1 reduce-scatter.1
where the time goes:
time: 637 us
  waiting for transfers between devices  301 us (47%)
  blocking collectives  163 us (26%)
  other arithmetic  125 us (20%)
  matrix products  19.8 us (3%)
  between operations  14.2 us (2%)
  local copies, waits for them, and re-layouts  13.6 us (2%)
    psum x1, waiting for transfers between devices, body(): lax.psum(picked(spectra, src_ids[step_no]).astype(jnp.bfloat16), 'chan')  289 us
    psum x1, blocking collectives, body(): totals = lax.psum(owned, 'freq')  93.4 us
    unnamed x1, blocking collectives  69.6 us
    scatter-add x2, other arithmetic, body(): jax.ops.segment_sum(jnp.ones((bin_ids.shape[0],), jnp.float32), bin_ids,...  57.6 us
    scatter-add x2, other arithmetic, body(): jax.ops.segment_sum(traces, bin_ids, num_segments=bin_total)  46.4 us
  transfers between devices with their start and end apart: 2, of which 2 were waited for; matrix products, arithmetic and copies ran while one was open for 11% of the time, Pallas kernels for 0%

commit v1 on v0

v1 whole, which is shorter than its diff:
```python
import math

import jax
import jax.numpy as jnp
from jax import lax
from jax.experimental import pallas as pl
from jax.experimental.pallas import tpu as pltpu
from jax.sharding import PartitionSpec as P

F = 1024
NLAG = 256
NBIN = 1024
W = 30
T = 2
NS = 32
FD = 64
C = 128
MESH = pl.DeviceIdType.MESH
BF = jnp.bfloat16
F32 = jnp.float32
NT = (((1,), (1,)), ((), ()))


def lag_basis(anchor, amount, totals, lag_count, windows):
    frequency = anchor + lax.iota(jnp.int32, amount)
    shifts = lax.iota(jnp.int32, lag_count) - lag_count // 2
    phases = frequency[:, None] * shifts[None, :] % (2 * totals)
    angles = phases.astype(jnp.float32) * (math.pi / totals)
    factor = 1.0 / math.sqrt(windows * totals)
    return jnp.concatenate([jnp.cos(angles), -jnp.sin(angles)], axis=0) * factor


def kernel(
    src_ref, spec_hbm, pair_ref, slot_ref, basis_ref, out_ref,
    spec, xf, bw, picker, pk, ck, rk, sk, slots, onehot, cnt, xs, xt, acc,
    bs, bc, br, lag, xr, zsum, zr, fin,
    in_sem, ck_s, ck_r, rk_s, rk_r, ag_s, ag_r, sc_s, sc_r,
    bc_s, bc_r, br_s, br_r, xr_s, xr_r, zr_s, zr_r, fx_s, fx_r,
):
    chan = lax.axis_index("chan")
    freq = lax.axis_index("freq")
    q = lax.div(chan, 2)
    k = lax.rem(chan, 2)
    y, z = lax.div(q, 4), lax.rem(q, 4)
    h, x = lax.div(freq, 4), lax.rem(freq, 4)
    core = {"chan": q * 2 + 1 - k, "freq": freq}

    def chip_at(o):
        return lax.rem(y + lax.div(o, 4), 4) * 4 + lax.rem(z + lax.rem(o, 4), 4)

    def chip_dev(o):
        return {"chan": chip_at(o) * 2 + k, "freq": freq}

    def x_dev(o):
        return {"chan": chan, "freq": h * 4 + lax.rem(x + o, 4)}

    def z_dev(o):
        return {"chan": chan, "freq": lax.rem(h + o, 4) * 4 + x}

    barrier = pltpu.get_barrier_semaphore()

    def greet(dev):
        pl.semaphore_signal(barrier, inc=1, device_id=dev, device_id_type=MESH)

    @pl.loop(1, 4)
    def _(o):
        greet(z_dev(o))
        greet(x_dev(o))

    @pl.loop(1, 16)
    def _(o):
        greet(chip_dev(o))

    greet(core)

    fetch = pltpu.make_async_copy(spec_hbm, spec, in_sem)
    fetch.start()

    lane = lax.broadcasted_iota(jnp.int32, (1, C), 1) + chan * C
    for t in range(T):
        for s in range(NS):
            row = t * NS + s
            picker[row : row + 1, :] = jnp.where(lane == src_ref[t, s], 1.0, 0.0)
    for part in range(2):
        xf[(part * 32 + W) * FD : (part + 1) * 32 * FD, :] = jnp.zeros((2 * FD, C), F32)
    fetch.wait()

    @pl.loop(0, W)
    def _(w):
        for part in range(2):
            at = pl.multiple_of((part * 32 + w) * FD, FD)
            xf[pl.ds(at, FD), :] = spec[part, w].astype(F32)

    pick = picker[...].astype(BF)

    @pl.loop(0, 32)
    def _(fp):
        for par in range(2):
            b = xf[pl.ds(par * 32 + fp, 64, stride=FD), :]
            bw[fp, par * 64 : par * 64 + 64, :C] = b.astype(BF)
            turned = jnp.concatenate([b[32:], -b[:32]], axis=0)
            bw[fp, par * 64 : par * 64 + 64, C:] = turned.astype(BF)
        got = lax.dot_general(pick, bw[fp, :, :C], NT, preferred_element_type=F32).astype(BF)
        for t in range(T):
            pk[t, fp] = got[t * NS : (t + 1) * NS]

    pl.semaphore_wait(barrier, 22)

    def core_src(t):
        return pltpu.make_async_remote_copy(
            src_ref=pk.at[t, pl.ds((1 - k) * 16, 16)], dst_ref=ck.at[t],
            send_sem=ck_s.at[t], recv_sem=ck_r.at[t], device_id=core, device_id_type=MESH)

    def scatter_src(t, o):
        return pltpu.make_async_remote_copy(
            src_ref=pk.at[t, k * 16 + chip_at(o)], dst_ref=rk.at[t, o],
            send_sem=rk_s.at[t, o], recv_sem=rk_r.at[t, o], device_id=chip_dev(o), device_id_type=MESH)

    def gather_src(t, o):
        return pltpu.make_async_remote_copy(
            src_ref=sk.at[t, k * 16 + q], dst_ref=sk.at[t, k * 16 + q],
            send_sem=ag_s.at[t, o], recv_sem=ag_r.at[t, o], device_id=chip_dev(o), device_id_type=MESH)

    def share_src(t):
        half = sk.at[t, pl.ds(k * 16, 16)]
        return pltpu.make_async_remote_copy(
            src_ref=half, dst_ref=half,
            send_sem=sc_s.at[t], recv_sem=sc_r.at[t], device_id=core, device_id_type=MESH)

    for t in range(T):
        core_src(t).start()
    for t in range(T):
        core_src(t).wait_recv()
        mine = pl.ds(k * 16, 16)
        pk[t, mine] = pk[t, mine] + ck[t]

        @pl.loop(1, 16)
        def _(o):
            scatter_src(t, o).start()

    bin_at = lax.broadcasted_iota(jnp.int32, (NBIN, 2 * C), 0)
    high = lax.broadcasted_iota(jnp.int32, (NBIN, 2 * C), 1) < C
    digits = jnp.where(high, lax.div(bin_at, 32), lax.rem(bin_at, 32)).astype(F32).astype(BF)

    @pl.loop(0, NBIN // C)
    def _(rb):
        rows = lax.broadcasted_iota(jnp.int32, (C, C), 0) + rb * C
        hit = jnp.concatenate(
            [jnp.where(slot_ref[i : i + 1, :] == rows, 1.0, 0.0).astype(BF) for i in range(NBIN // C)], axis=1)
        found = jnp.dot(hit, digits, preferred_element_type=F32)
        at = pl.ds(pl.multiple_of(rb * C, C), C)
        slots[at, :] = (found[:, :C] * 32.0 + found[:, C:]).astype(jnp.int32)
        cnt[at, :] = jnp.zeros((C, C), F32)

    def build_hits(t):
        @pl.loop(0, 4)
        def _(ch):
            @pl.loop(0, NBIN // C)
            def _(rb):
                at = pl.ds(pl.multiple_of(rb * C, C), C)
                held = slots[at, :]
                total = cnt[at, :]
                for i in range(8):
                    row = pair_ref[pl.ds(t * NS + ch * 8 + i, 1), :]
                    hit = jnp.where(held == row, 1.0, 0.0)
                    onehot[t * 4 + ch, at, i * C : (i + 1) * C] = hit.astype(BF)
                    total = total + hit
                cnt[at, :] = total

    def reduce_src(t):
        total = pk[t, k * 16 + q]
        for o in range(1, 16):
            scatter_src(t, o).wait_recv()
            total = total + rk[t, o]
        sk[t, k * 16 + q] = total

        @pl.loop(1, 16)
        def _(o):
            gather_src(t, o).start()

    build_hits(0)
    reduce_src(0)
    reduce_src(1)
    build_hits(1)

    sums = jnp.dot(cnt[...].astype(BF), jnp.ones((C, C), BF), preferred_element_type=F32)
    diagonal = lax.broadcasted_iota(jnp.int32, (32, C), 0) == lax.broadcasted_iota(jnp.int32, (32, C), 1)
    for owner in range(32):
        line = jnp.sum(jnp.where(diagonal, sums[owner * 32 : owner * 32 + 32], 0.0), axis=0, keepdims=True)
        bs[owner % 2, owner // 2, 32:40, :] = jnp.broadcast_to(line, (8, C))

    first = lax.broadcasted_iota(jnp.int32, (NS, C), 1) < 64

    def cross(t, fp):
        a = sk[t, fp]
        zero = jnp.zeros_like(a)
        lhs = jnp.concatenate([jnp.where(first, a, zero), jnp.where(first, zero, a)], axis=0)
        got = jnp.dot(lhs, bw[fp], preferred_element_type=F32)
        for par in range(2):
            for j in range(2):
                xs[pl.ds(j * FD + par * 32 + fp, NS, stride=2 * FD), :] = (
                    got[par * NS : (par + 1) * NS, j * C : (j + 1) * C])

    for t in range(T):
        @pl.loop(1, 16)
        def _(o):
            gather_src(t, o).wait_recv()

        share_src(t).start()

        @pl.loop(0, 16)
        def _(i):
            cross(t, k * 16 + i)

        share_src(t).wait_recv()

        @pl.loop(0, 16)
        def _(i):
            cross(t, (1 - k) * 16 + i)

        @pl.loop(0, 4)
        def _(ch):
            for i in range(8):
                at = pl.multiple_of((ch * 8 + i) * 2 * FD, 2 * FD)
                v = xs[pl.ds(at, 2 * FD), :]
                hi = v.astype(BF)
                xt[ch, :C, i * C : (i + 1) * C] = hi
                xt[ch, C:, i * C : (i + 1) * C] = (v - hi.astype(F32)).astype(BF)

        @pl.loop(0, 4)
        def _(ch):
            got = lax.dot_general(onehot[t * 4 + ch], xt[ch], NT, preferred_element_type=F32)
            if t == 0:
                @pl.when(ch == 0)
                def _():
                    acc[...] = got

                @pl.when(ch > 0)
                def _():
                    acc[...] += got
            else:
                acc[...] += got

    for owner in range(32):
        at = owner * 32
        bs[owner % 2, owner // 2, :32, :] = acc[at : at + 32, :C] + acc[at : at + 32, C:]

    core_bins = pltpu.make_async_remote_copy(
        src_ref=bs.at[1 - k], dst_ref=bc, send_sem=bc_s, recv_sem=bc_r, device_id=core, device_id_type=MESH)
    core_bins.start()
    core_bins.wait_recv()
    bs[k] = bs[k] + bc[...]

    def scatter_bins(o):
        return pltpu.make_async_remote_copy(
            src_ref=bs.at[k, chip_at(o)], dst_ref=br.at[o],
            send_sem=br_s.at[o], recv_sem=br_r.at[o], device_id=chip_dev(o), device_id_type=MESH)

    @pl.loop(1, 16)
    def _(o):
        scatter_bins(o).start()

    total = bs[k, q]
    for o in range(1, 16):
        scatter_bins(o).wait_recv()
        total = total + br[o]

    traces = jnp.dot(total[:32], basis_ref[...], precision=lax.Precision.HIGHEST, preferred_element_type=F32)
    for part in range(4):
        lag[part] = traces[part * 8 : part * 8 + 8]

    def scatter_x(o):
        return pltpu.make_async_remote_copy(
            src_ref=lag.at[lax.rem(x + o, 4)], dst_ref=xr.at[o],
            send_sem=xr_s.at[o], recv_sem=xr_r.at[o], device_id=x_dev(o), device_id_type=MESH)

    def swap_z(o):
        return pltpu.make_async_remote_copy(
            src_ref=zsum, dst_ref=zr.at[o],
            send_sem=zr_s.at[o], recv_sem=zr_r.at[o], device_id=z_dev(o), device_id_type=MESH)

    def gather_x(o):
        return pltpu.make_async_remote_copy(
            src_ref=fin.at[x], dst_ref=fin.at[x],
            send_sem=fx_s.at[o], recv_sem=fx_r.at[o], device_id=x_dev(o), device_id_type=MESH)

    for o in range(1, 4):
        scatter_x(o).start()
    rows = lag[x]
    for o in range(1, 4):
        scatter_x(o).wait_recv()
        rows = rows + xr[o]
    zsum[...] = rows
    for o in range(1, 4):
        swap_z(o).start()
    owned = (lax.broadcasted_iota(jnp.int32, (8, C), 1)
             == lax.broadcasted_iota(jnp.int32, (8, C), 0) + x * 8)
    counts = jnp.sum(jnp.where(owned, total[32:40], 0.0), axis=1, keepdims=True)
    norm = jnp.sqrt(jnp.maximum(counts, 1.0))
    for o in range(1, 4):
        swap_z(o).wait_recv()
        rows = rows + zr[o]
    fin[x] = rows / norm
    for o in range(1, 4):
        gather_x(o).start()

    for t in range(T):
        core_src(t).wait_send()
        share_src(t).wait_send()

        @pl.loop(1, 16)
        def _(o):
            scatter_src(t, o).wait_send()
            gather_src(t, o).wait_send()

    core_bins.wait_send()

    @pl.loop(1, 16)
    def _(o):
        scatter_bins(o).wait_send()

    for o in range(1, 4):
        scatter_x(o).wait_send()
        swap_z(o).wait_send()
    for o in range(1, 4):
        gather_x(o).wait()
    out_ref[...] = fin[...]


def body(spectra, src_ids, pair_bin, slot_of_bin):
    basis = lag_basis(lax.axis_index("freq") * FD, FD, F, NLAG, W)
    vmem = pl.BlockSpec(memory_space=pltpu.VMEM)
    dma = pltpu.SemaphoreType.DMA
    out = pl.pallas_call(
        kernel,
        out_shape=jax.ShapeDtypeStruct((4, 8, NLAG), F32),
        in_specs=[pl.BlockSpec(memory_space=pltpu.SMEM), pl.BlockSpec(memory_space=pl.ANY), vmem, vmem, vmem],
        out_specs=vmem,
        scratch_shapes=[
            pltpu.VMEM((2, W, FD, C), BF),
            pltpu.VMEM((64 * FD, C), F32),
            pltpu.VMEM((32, 2 * 64, 2 * C), BF),
            pltpu.VMEM((T * NS, C), F32),
            pltpu.VMEM((T, 32, NS, C), BF),
            pltpu.VMEM((T, 16, NS, C), BF),
            pltpu.VMEM((T, 16, NS, C), BF),
            pltpu.VMEM((T, 32, NS, C), BF),
            pltpu.VMEM((NBIN, C), jnp.int32),
            pltpu.VMEM((8, NBIN, 8 * C), BF),
            pltpu.VMEM((NBIN, C), F32),
            pltpu.VMEM((NS * 2 * FD, C), F32),
            pltpu.VMEM((4, 2 * C, 8 * C), BF),
            pltpu.VMEM((NBIN, 2 * C), F32),
            pltpu.VMEM((2, 16, 40, C), F32),
            pltpu.VMEM((16, 40, C), F32),
            pltpu.VMEM((16, 40, C), F32),
            pltpu.VMEM((4, 8, NLAG), F32),
            pltpu.VMEM((4, 8, NLAG), F32),
            pltpu.VMEM((8, NLAG), F32),
            pltpu.VMEM((4, 8, NLAG), F32),
            pltpu.VMEM((4, 8, NLAG), F32),
            dma, dma((T,)), dma((T,)), dma((T, 16)), dma((T, 16)), dma((T, 16)), dma((T, 16)), dma((T,)), dma((T,)),
            dma, dma, dma((16,)), dma((16,)), dma((4,)), dma((4,)), dma((4,)), dma((4,)), dma((4,)), dma((4,)),
        ],
        compiler_params=pltpu.CompilerParams(
            collective_id=0, has_side_effects=True, vmem_limit_bytes=56 * 1024 * 1024),
    )(src_ids, spectra, pair_bin.reshape(T * NS, C), slot_of_bin.reshape(NBIN // C, C), basis)
    return out.reshape(32, NLAG)


def solution(mesh):
    return jax.shard_map(
        body,
        mesh=mesh,
        in_specs=(P(None, None, "freq", "chan"), P(), P(None, None, "chan"), P()),
        out_specs=P("chan", None),
        check_vma=False,
    )
```

time: 637 us -> 83.8 us (0.13)
  the two profiles are of different devices: /device:TPU:128 before, /device:TPU:24 now
where the time goes in v1:
time: 83.8 us; the launch traced here: 83.6 us
  Pallas kernels  81.2 us (97%)
  local copies, waits for them, and re-layouts  1.38 us (2%)
  other arithmetic  1.01 us (1%)
    pallas_call x1, Pallas kernels, body(): pl.pallas_call(kernel, out_shape=jax.ShapeDtypeStruct((4, 8, NLAG), F32),...  81.2 us

profile of v1, /device:TPU:24, one launch (start us, length us, event | category | flops | bytes accessed | tf_op | source)
XLA Modules:
  0.0 83.6 jit_solution(15848137545441826838)
XLA Ops:
  0.0 0.3 fusion.3
  0.4 0.7 maximum_multiply_fusion.basis_ref
  1.0 81.2 %shard_map.46 = f32[4,8,256]{2,1,0:T(8,128)} custom-call(s32[2,32]{1,0:T(2,128)} %src_ref.1, bf16[2,30,64,128]{3,2,1,0:T(8,128)(2,1)} %spec_hbm.1, s32[64,128]{1,0:T(8,128)} %bitcast.4, s32[8,128]{1,0:T(8,128)} %bitcast.5, f32[128,256]{1,0:T(8,128)} %maximum_multiply_fusion.basis_ref), custom_call_target="tpu_custom_call" | custom-call | tf_op jit(solution)/shard_map/pallas_call | solution.py:334
  82.2 1.4 %copy.6 = f32[32,256]{1,0:T(8,128)} copy(f32[32,256]{1,0:T(8,128)} %bitcast.3) | data formatting | bytes 65536
  (2 shorter events, 0.0 us)

commit v2 on v1

--- a/solution.py
+++ b/solution.py
@@ -21,18 +21,9 @@
 NT = (((1,), (1,)), ((), ()))
 
 
-def lag_basis(anchor, amount, totals, lag_count, windows):
-    frequency = anchor + lax.iota(jnp.int32, amount)
-    shifts = lax.iota(jnp.int32, lag_count) - lag_count // 2
-    phases = frequency[:, None] * shifts[None, :] % (2 * totals)
-    angles = phases.astype(jnp.float32) * (math.pi / totals)
-    factor = 1.0 / math.sqrt(windows * totals)
-    return jnp.concatenate([jnp.cos(angles), -jnp.sin(angles)], axis=0) * factor
-
-
 def kernel(
-    src_ref, spec_hbm, pair_ref, slot_ref, basis_ref, out_ref,
-    spec, xf, bw, picker, pk, ck, rk, sk, slots, onehot, cnt, xs, xt, acc,
+    src_ref, spec_hbm, pair_ref, slot_ref, out_ref, norm_ref,
+    spec, xf, bw, bt, picker, pk, ck, rk, sk, slots, onehot, cnt, xs, xt, basis,
     bs, bc, br, lag, xr, zsum, zr, fin,
     in_sem, ck_s, ck_r, rk_s, rk_r, ag_s, ag_r, sc_s, sc_r,
     bc_s, bc_r, br_s, br_r, xr_s, xr_r, zr_s, zr_r, fx_s, fx_r,
@@ -48,6 +39,9 @@
     def chip_at(o):
         return lax.rem(y + lax.div(o, 4), 4) * 4 + lax.rem(z + lax.rem(o, 4), 4)
 
+    def chip_from(o):
+        return lax.rem(y + 4 - lax.div(o, 4), 4) * 4 + lax.rem(z + 4 - lax.rem(o, 4), 4)
+
     def chip_dev(o):
         return {"chan": chip_at(o) * 2 + k, "freq": freq}
 
@@ -85,7 +79,7 @@
         xf[(part * 32 + W) * FD : (part + 1) * 32 * FD, :] = jnp.zeros((2 * FD, C), F32)
     fetch.wait()
 
-    @pl.loop(0, W)
+    @pl.loop(0, W, unroll=5)
     def _(w):
         for part in range(2):
             at = pl.multiple_of((part * 32 + w) * FD, FD)
@@ -93,14 +87,12 @@
 
     pick = picker[...].astype(BF)
 
-    @pl.loop(0, 32)
+    @pl.loop(0, 32, unroll=8)
     def _(fp):
-        for par in range(2):
-            b = xf[pl.ds(par * 32 + fp, 64, stride=FD), :]
-            bw[fp, par * 64 : par * 64 + 64, :C] = b.astype(BF)
-            turned = jnp.concatenate([b[32:], -b[:32]], axis=0)
-            bw[fp, par * 64 : par * 64 + 64, C:] = turned.astype(BF)
-        got = lax.dot_general(pick, bw[fp, :, :C], NT, preferred_element_type=F32).astype(BF)
+        halves = [xf[pl.ds(par * 32 + fp, 64, stride=FD), :].astype(BF) for par in range(2)]
+        b = jnp.concatenate(halves, axis=0)
+        bw[fp] = b
+        got = lax.dot_general(pick, b, NT, preferred_element_type=F32).astype(BF)
         for t in range(T):
             pk[t, fp] = got[t * NS : (t + 1) * NS]
 
@@ -121,11 +113,11 @@
             src_ref=sk.at[t, k * 16 + q], dst_ref=sk.at[t, k * 16 + q],
             send_sem=ag_s.at[t, o], recv_sem=ag_r.at[t, o], device_id=chip_dev(o), device_id_type=MESH)
 
-    def share_src(t):
-        half = sk.at[t, pl.ds(k * 16, 16)]
-        return pltpu.make_async_remote_copy(
-            src_ref=half, dst_ref=half,
-            send_sem=sc_s.at[t], recv_sem=sc_r.at[t], device_id=core, device_id_type=MESH)
+    def share_src(t, o, half):
+        at = half * 16 + chip_from(o)
+        return pltpu.make_async_remote_copy(
+            src_ref=sk.at[t, at], dst_ref=sk.at[t, at],
+            send_sem=sc_s.at[t, o], recv_sem=sc_r.at[t, o], device_id=core, device_id_type=MESH)
 
     for t in range(T):
         core_src(t).start()
@@ -138,13 +130,21 @@
         def _(o):
             scatter_src(t, o).start()
 
+    @pl.loop(0, 32, unroll=4)
+    def _(fp):
+        for par in range(2):
+            at = par * 64
+            bt[fp, at : at + 32] = bw[fp, at + 32 : at + 64]
+            bt[fp, at + 32 : at + 64] = -bw[fp, at : at + 32]
+
     bin_at = lax.broadcasted_iota(jnp.int32, (NBIN, 2 * C), 0)
     high = lax.broadcasted_iota(jnp.int32, (NBIN, 2 * C), 1) < C
     digits = jnp.where(high, lax.div(bin_at, 32), lax.rem(bin_at, 32)).astype(F32).astype(BF)
 
     @pl.loop(0, NBIN // C)
     def _(rb):
-        rows = lax.broadcasted_iota(jnp.int32, (C, C), 0) + rb * C
+        at = lax.broadcasted_iota(jnp.int32, (C, C), 0) + rb * C
+        rows = lax.div(lax.rem(at, 512), 32) * 64 + lax.div(at, 512) * 32 + lax.rem(at, 32)
         hit = jnp.concatenate(
             [jnp.where(slot_ref[i : i + 1, :] == rows, 1.0, 0.0).astype(BF) for i in range(NBIN // C)], axis=1)
         found = jnp.dot(hit, digits, preferred_element_type=F32)
@@ -187,7 +187,14 @@
     diagonal = lax.broadcasted_iota(jnp.int32, (32, C), 0) == lax.broadcasted_iota(jnp.int32, (32, C), 1)
     for owner in range(32):
         line = jnp.sum(jnp.where(diagonal, sums[owner * 32 : owner * 32 + 32], 0.0), axis=0, keepdims=True)
-        bs[owner % 2, owner // 2, 32:40, :] = jnp.broadcast_to(line, (8, C))
+        bs[owner // 16, owner % 16, 32:40, :] = jnp.broadcast_to(line, (8, C))
+
+    tone = lax.broadcasted_iota(jnp.int32, (FD, NLAG), 0) + freq * FD
+    shift = lax.broadcasted_iota(jnp.int32, (FD, NLAG), 1) - NLAG // 2
+    angles = ((tone * shift) & (2 * F - 1)).astype(F32) * (math.pi / F)
+    factor = 1.0 / math.sqrt(W * F)
+    basis[:FD, :] = jnp.cos(angles) * factor
+    basis[FD:, :] = -jnp.sin(angles) * factor
 
     first = lax.broadcasted_iota(jnp.int32, (NS, C), 1) < 64
 
@@ -195,59 +202,52 @@
         a = sk[t, fp]
         zero = jnp.zeros_like(a)
         lhs = jnp.concatenate([jnp.where(first, a, zero), jnp.where(first, zero, a)], axis=0)
-        got = jnp.dot(lhs, bw[fp], preferred_element_type=F32)
+        got = jnp.dot(lhs, jnp.concatenate([bw[fp], bt[fp]], axis=1), preferred_element_type=F32)
         for par in range(2):
             for j in range(2):
                 xs[pl.ds(j * FD + par * 32 + fp, NS, stride=2 * FD), :] = (
                     got[par * NS : (par + 1) * NS, j * C : (j + 1) * C])
 
-    for t in range(T):
-        @pl.loop(1, 16)
-        def _(o):
-            gather_src(t, o).wait_recv()
-
-        share_src(t).start()
-
-        @pl.loop(0, 16)
-        def _(i):
-            cross(t, k * 16 + i)
-
-        share_src(t).wait_recv()
-
-        @pl.loop(0, 16)
-        def _(i):
-            cross(t, (1 - k) * 16 + i)
-
-        @pl.loop(0, 4)
-        def _(ch):
+    core_bins = pltpu.make_async_remote_copy(
+        src_ref=bs.at[1 - k], dst_ref=bc, send_sem=bc_s, recv_sem=bc_r, device_id=core, device_id_type=MESH)
+
+    for t in range(T):
+        share_src(t, 0, k).start()
+        for group in range(4):
+            members = range(group * 4, group * 4 + 4)
+            for o in members:
+                if o > 0:
+                    gather_src(t, o).wait_recv()
+                    share_src(t, o, k).start()
+            for o in members:
+                cross(t, k * 16 + chip_from(o))
+        for group in range(2):
+            members = range(group * 8, group * 8 + 8)
+            for o in members:
+                share_src(t, o, 1 - k).wait_recv()
+            for o in members:
+                cross(t, (1 - k) * 16 + chip_from(o))
+
+        for ch in range(4):
             for i in range(8):
-                at = pl.multiple_of((ch * 8 + i) * 2 * FD, 2 * FD)
-                v = xs[pl.ds(at, 2 * FD), :]
+                at = (ch * 8 + i) * 2 * FD
+                v = xs[at : at + 2 * FD, :]
                 hi = v.astype(BF)
                 xt[ch, :C, i * C : (i + 1) * C] = hi
                 xt[ch, C:, i * C : (i + 1) * C] = (v - hi.astype(F32)).astype(BF)
 
-        @pl.loop(0, 4)
-        def _(ch):
-            got = lax.dot_general(onehot[t * 4 + ch], xt[ch], NT, preferred_element_type=F32)
+        for half in (1 - k, k):
+            at = pl.ds(pl.multiple_of(half * 512, 512), 512)
+            got = sum(
+                lax.dot_general(onehot[t * 4 + ch, at, :], xt[ch], NT, preferred_element_type=F32) for ch in range(4))
+            part = (got[:, :C] + got[:, C:]).reshape(16, 32, C)
             if t == 0:
-                @pl.when(ch == 0)
-                def _():
-                    acc[...] = got
-
-                @pl.when(ch > 0)
-                def _():
-                    acc[...] += got
+                bs[half, :, :32, :] = part
             else:
-                acc[...] += got
-
-    for owner in range(32):
-        at = owner * 32
-        bs[owner % 2, owner // 2, :32, :] = acc[at : at + 32, :C] + acc[at : at + 32, C:]
-
-    core_bins = pltpu.make_async_remote_copy(
-        src_ref=bs.at[1 - k], dst_ref=bc, send_sem=bc_s, recv_sem=bc_r, device_id=core, device_id_type=MESH)
-    core_bins.start()
+                bs[half, :, :32, :] = bs[half, :, :32, :] + part
+                if half is not k:
+                    core_bins.start()
+
     core_bins.wait_recv()
     bs[k] = bs[k] + bc[...]
 
@@ -265,7 +265,7 @@
         scatter_bins(o).wait_recv()
         total = total + br[o]
 
-    traces = jnp.dot(total[:32], basis_ref[...], precision=lax.Precision.HIGHEST, preferred_element_type=F32)
+    traces = jnp.dot(total[:32], basis[...], precision=lax.Precision.HIGHEST, preferred_element_type=F32)
     for part in range(4):
         lag[part] = traces[part * 8 : part * 8 + 8]
 
@@ -293,23 +293,22 @@
     zsum[...] = rows
     for o in range(1, 4):
         swap_z(o).start()
-    owned = (lax.broadcasted_iota(jnp.int32, (8, C), 1)
-             == lax.broadcasted_iota(jnp.int32, (8, C), 0) + x * 8)
-    counts = jnp.sum(jnp.where(owned, total[32:40], 0.0), axis=1, keepdims=True)
-    norm = jnp.sqrt(jnp.maximum(counts, 1.0))
+    counts = jnp.sum(jnp.where(diagonal, total[32:33], 0.0), axis=1, keepdims=True)
+    norm_ref[...] = jnp.broadcast_to(jnp.sqrt(jnp.maximum(counts, 1.0)), (32, NLAG))
     for o in range(1, 4):
         swap_z(o).wait_recv()
         rows = rows + zr[o]
-    fin[x] = rows / norm
+    fin[x] = rows
     for o in range(1, 4):
         gather_x(o).start()
 
     for t in range(T):
         core_src(t).wait_send()
-        share_src(t).wait_send()
+        share_src(t, 0, k).wait_send()
 
         @pl.loop(1, 16)
         def _(o):
+            share_src(t, o, k).wait_send()
             scatter_src(t, o).wait_send()
             gather_src(t, o).wait_send()
 
@@ -328,18 +327,18 @@
 
 
 def body(spectra, src_ids, pair_bin, slot_of_bin):
-    basis = lag_basis(lax.axis_index("freq") * FD, FD, F, NLAG, W)
     vmem = pl.BlockSpec(memory_space=pltpu.VMEM)
     dma = pltpu.SemaphoreType.DMA
-    out = pl.pallas_call(
+    sums, norm = pl.pallas_call(
         kernel,
-        out_shape=jax.ShapeDtypeStruct((4, 8, NLAG), F32),
-        in_specs=[pl.BlockSpec(memory_space=pltpu.SMEM), pl.BlockSpec(memory_space=pl.ANY), vmem, vmem, vmem],
-        out_specs=vmem,
+        out_shape=[jax.ShapeDtypeStruct((4, 8, NLAG), F32), jax.ShapeDtypeStruct((32, NLAG), F32)],
+        in_specs=[pl.BlockSpec(memory_space=pltpu.SMEM), pl.BlockSpec(memory_space=pl.ANY), vmem, vmem],
+        out_specs=[vmem, vmem],
         scratch_shapes=[
             pltpu.VMEM((2, W, FD, C), BF),
             pltpu.VMEM((64 * FD, C), F32),
-            pltpu.VMEM((32, 2 * 64, 2 * C), BF),
+            pltpu.VMEM((32, 2 * 64, C), BF),
+            pltpu.VMEM((32, 2 * 64, C), BF),
             pltpu.VMEM((T * NS, C), F32),
             pltpu.VMEM((T, 32, NS, C), BF),
             pltpu.VMEM((T, 16, NS, C), BF),
@@ -350,7 +349,7 @@
             pltpu.VMEM((NBIN, C), F32),
             pltpu.VMEM((NS * 2 * FD, C), F32),
             pltpu.VMEM((4, 2 * C, 8 * C), BF),
-            pltpu.VMEM((NBIN, 2 * C), F32),
+            pltpu.VMEM((2 * FD, NLAG), F32),
             pltpu.VMEM((2, 16, 40, C), F32),
             pltpu.VMEM((16, 40, C), F32),
             pltpu.VMEM((16, 40, C), F32),
@@ -359,13 +358,13 @@
             pltpu.VMEM((8, NLAG), F32),
             pltpu.VMEM((4, 8, NLAG), F32),
             pltpu.VMEM((4, 8, NLAG), F32),
-            dma, dma((T,)), dma((T,)), dma((T, 16)), dma((T, 16)), dma((T, 16)), dma((T, 16)), dma((T,)), dma((T,)),
+            dma, dma((T,)), dma((T,)), dma((T, 16)), dma((T, 16)), dma((T, 16)), dma((T, 16)), dma((T, 16)), dma((T, 16)),
             dma, dma, dma((16,)), dma((16,)), dma((4,)), dma((4,)), dma((4,)), dma((4,)), dma((4,)), dma((4,)),
         ],
         compiler_params=pltpu.CompilerParams(
             collective_id=0, has_side_effects=True, vmem_limit_bytes=56 * 1024 * 1024),
-    )(src_ids, spectra, pair_bin.reshape(T * NS, C), slot_of_bin.reshape(NBIN // C, C), basis)
-    return out.reshape(32, NLAG)
+    )(src_ids, spectra, pair_bin.reshape(T * NS, C), slot_of_bin.reshape(NBIN // C, C))
+    return sums.reshape(32, NLAG) / norm
 
 
 def solution(mesh):

time: 83.8 us -> 70 us (0.84)
  the two profiles are of different devices: /device:TPU:24 before, /device:TPU:4 now
where the time goes in v2:
time: 70 us; the launch traced here: 69.7 us
  Pallas kernels  68.3 us (98%)
  other arithmetic  1.4 us (2%)
    pallas_call x1, Pallas kernels, body(): pl.pallas_call(kernel, out_shape=[jax.ShapeDtypeStruct((4, 8, NLAG), F32)...  68.3 us
    div x1, other arithmetic, body(): return sums.reshape(32, NLAG) / norm  1.4 us

profile of v2, /device:TPU:4, one launch (start us, length us, event | category | flops | bytes accessed | tf_op | source)
XLA Modules:
  0.0 69.7 jit_solution(7195109553623823385)
XLA Ops:
  0.0 68.3 %shard_map.46 = (f32[4,8,256]{2,1,0:T(8,128)}, f32[32,256]{1,0:T(8,128)}) custom-call(s32[2,32]{1,0:T(2,128)} %src_ref.1, bf16[2,30,64,128]{3,2,1,0:T(8,128)(2,1)} %spec_hbm.1, s32[64,128]{1,0:T(8,128)} %bitcast.4, s32[8,128]{1,0:T(8,128)} %bitcast.5), custom_call_target="tpu_custom_call" | custom-call | tf_op jit(solution)/shard_map/pallas_call | solution.py:332
  68.3 1.4 %bitcast_divide_fusion = f32[32,256]{1,0:T(8,128)} fusion(f32[32,256]{1,0:T(8,128)} %get-tuple-element.8, f32[4,8,256]{2,1,0:T(8,128)} %get-tuple-element.7), kind=kLoop, calls=%fused_computation | loop fusion | flops 8192 | bytes 98304 | tf_op jit(solution)/shard_map/div | solution.py:367

commit v3 on v2

--- a/solution.py
+++ b/solution.py
@@ -144,13 +144,14 @@
     @pl.loop(0, NBIN // C)
     def _(rb):
         at = lax.broadcasted_iota(jnp.int32, (C, C), 0) + rb * C
-        rows = lax.div(lax.rem(at, 512), 32) * 64 + lax.div(at, 512) * 32 + lax.rem(at, 32)
+        chip = lax.div(lax.rem(at, 256), 32) * 2 + lax.div(lax.rem(at, 512), 256)
+        rows = chip * 64 + lax.div(at, 512) * 32 + lax.rem(at, 32)
         hit = jnp.concatenate(
             [jnp.where(slot_ref[i : i + 1, :] == rows, 1.0, 0.0).astype(BF) for i in range(NBIN // C)], axis=1)
         found = jnp.dot(hit, digits, preferred_element_type=F32)
         at = pl.ds(pl.multiple_of(rb * C, C), C)
         slots[at, :] = (found[:, :C] * 32.0 + found[:, C:]).astype(jnp.int32)
-        cnt[at, :] = jnp.zeros((C, C), F32)
+        cnt[at, :] = jnp.zeros((C, C), BF)
 
     def build_hits(t):
         @pl.loop(0, 4)
@@ -162,8 +163,8 @@
                 total = cnt[at, :]
                 for i in range(8):
                     row = pair_ref[pl.ds(t * NS + ch * 8 + i, 1), :]
-                    hit = jnp.where(held == row, 1.0, 0.0)
-                    onehot[t * 4 + ch, at, i * C : (i + 1) * C] = hit.astype(BF)
+                    hit = jnp.where(held == row, 1.0, 0.0).astype(BF)
+                    onehot[t * 4 + ch, at, i * C : (i + 1) * C] = hit
                     total = total + hit
                 cnt[at, :] = total
 
@@ -183,18 +184,11 @@
     reduce_src(1)
     build_hits(1)
 
-    sums = jnp.dot(cnt[...].astype(BF), jnp.ones((C, C), BF), preferred_element_type=F32)
+    sums = jnp.dot(cnt[...], jnp.ones((C, C), BF), preferred_element_type=F32)
     diagonal = lax.broadcasted_iota(jnp.int32, (32, C), 0) == lax.broadcasted_iota(jnp.int32, (32, C), 1)
     for owner in range(32):
         line = jnp.sum(jnp.where(diagonal, sums[owner * 32 : owner * 32 + 32], 0.0), axis=0, keepdims=True)
-        bs[owner // 16, owner % 16, 32:40, :] = jnp.broadcast_to(line, (8, C))
-
-    tone = lax.broadcasted_iota(jnp.int32, (FD, NLAG), 0) + freq * FD
-    shift = lax.broadcasted_iota(jnp.int32, (FD, NLAG), 1) - NLAG // 2
-    angles = ((tone * shift) & (2 * F - 1)).astype(F32) * (math.pi / F)
-    factor = 1.0 / math.sqrt(W * F)
-    basis[:FD, :] = jnp.cos(angles) * factor
-    basis[FD:, :] = -jnp.sin(angles) * factor
+        bs[owner // 16, owner // 8 % 2, owner % 8, 32:33, :] = line
 
     first = lax.broadcasted_iota(jnp.int32, (NS, C), 1) < 64
 
@@ -208,26 +202,18 @@
                 xs[pl.ds(j * FD + par * 32 + fp, NS, stride=2 * FD), :] = (
                     got[par * NS : (par + 1) * NS, j * C : (j + 1) * C])
 
-    core_bins = pltpu.make_async_remote_copy(
-        src_ref=bs.at[1 - k], dst_ref=bc, send_sem=bc_s, recv_sem=bc_r, device_id=core, device_id_type=MESH)
-
-    for t in range(T):
-        share_src(t, 0, k).start()
-        for group in range(4):
-            members = range(group * 4, group * 4 + 4)
-            for o in members:
-                if o > 0:
-                    gather_src(t, o).wait_recv()
-                    share_src(t, o, k).start()
-            for o in members:
-                cross(t, k * 16 + chip_from(o))
-        for group in range(2):
-            members = range(group * 8, group * 8 + 8)
-            for o in members:
-                share_src(t, o, 1 - k).wait_recv()
-            for o in members:
-                cross(t, (1 - k) * 16 + chip_from(o))
-
+    def core_bins(g):
+        return pltpu.make_async_remote_copy(
+            src_ref=bs.at[1 - k, g], dst_ref=bc.at[g],
+            send_sem=bc_s.at[g], recv_sem=bc_r.at[g], device_id=core, device_id_type=MESH)
+
+    def scatter_bins(o):
+        to = chip_at(o)
+        return pltpu.make_async_remote_copy(
+            src_ref=bs.at[k, lax.rem(to, 2), lax.div(to, 2)], dst_ref=br.at[o],
+            send_sem=br_s.at[o], recv_sem=br_r.at[o], device_id=chip_dev(o), device_id_type=MESH)
+
+    def split(t):
         for ch in range(4):
             for i in range(8):
                 at = (ch * 8 + i) * 2 * FD
@@ -236,31 +222,78 @@
                 xt[ch, :C, i * C : (i + 1) * C] = hi
                 xt[ch, C:, i * C : (i + 1) * C] = (v - hi.astype(F32)).astype(BF)
 
-        for half in (1 - k, k):
-            at = pl.ds(pl.multiple_of(half * 512, 512), 512)
-            got = sum(
-                lax.dot_general(onehot[t * 4 + ch, at, :], xt[ch], NT, preferred_element_type=F32) for ch in range(4))
-            part = (got[:, :C] + got[:, C:]).reshape(16, 32, C)
-            if t == 0:
-                bs[half, :, :32, :] = part
-            else:
-                bs[half, :, :32, :] = bs[half, :, :32, :] + part
-                if half is not k:
-                    core_bins.start()
-
-    core_bins.wait_recv()
-    bs[k] = bs[k] + bc[...]
-
-    def scatter_bins(o):
-        return pltpu.make_async_remote_copy(
-            src_ref=bs.at[k, chip_at(o)], dst_ref=br.at[o],
-            send_sem=br_s.at[o], recv_sem=br_r.at[o], device_id=chip_dev(o), device_id_type=MESH)
+    def stack(t, start, rows):
+        at = pl.ds(start, rows)
+        got = sum(
+            lax.dot_general(onehot[t * 4 + ch, at, :], xt[ch], NT, preferred_element_type=F32) for ch in range(4))
+        return (got[:, :C] + got[:, C:]).reshape(rows // 32, 32, C)
+
+    share_src(0, 0, k).start()
+    for group in range(4):
+        members = range(group * 4, group * 4 + 4)
+        for o in members:
+            if o > 0:
+                gather_src(0, o).wait_recv()
+                share_src(0, o, k).start()
+        for o in members:
+            cross(0, k * 16 + chip_from(o))
+    for group in range(2):
+        members = range(group * 8, group * 8 + 8)
+        for o in members:
+            share_src(0, o, 1 - k).wait_recv()
+        for o in members:
+            cross(0, (1 - k) * 16 + chip_from(o))
+
+    share_src(1, 0, k).start()
 
     @pl.loop(1, 16)
     def _(o):
-        scatter_bins(o).start()
-
-    total = bs[k, q]
+        gather_src(1, o).wait_recv()
+        share_src(1, o, k).start()
+
+    split(0)
+    part = stack(0, 0, NBIN)
+    for n in range(4):
+        bs[n // 2, n % 2, :, :32, :] = part[n * 8 : n * 8 + 8]
+
+    for o in range(16):
+        cross(1, k * 16 + chip_from(o))
+
+    @pl.loop(0, 16)
+    def _(o):
+        share_src(1, o, 1 - k).wait_recv()
+
+    for o in range(16):
+        cross(1, (1 - k) * 16 + chip_from(o))
+    split(1)
+
+    def stack_on(half, g):
+        part = stack(1, pl.multiple_of(half * 512 + g * 256, 256), 256)
+        bs[half, g, :, :32, :] = bs[half, g, :, :32, :] + part
+
+    for g in range(2):
+        stack_on(1 - k, g)
+        core_bins(g).start()
+        stack_on(k, g)
+        core_bins(g).wait_recv()
+        bs[k, g] = bs[k, g] + bc[g]
+
+        @pl.loop(0, 8)
+        def _(n):
+            o = lax.div(n, 2) * 4 + lax.rem(n, 2) * 2 + lax.rem(z + g, 2)
+
+            @pl.when(o > 0)
+            def _():
+                scatter_bins(o).start()
+
+    tone = lax.broadcasted_iota(jnp.int32, (FD, NLAG), 0) + freq * FD
+    shift = lax.broadcasted_iota(jnp.int32, (FD, NLAG), 1) - NLAG // 2
+    angles = ((tone * shift) & (2 * F - 1)).astype(F32) * (math.pi / F)
+    factor = 1.0 / math.sqrt(W * F)
+    basis[:FD, :] = jnp.cos(angles) * factor
+    basis[FD:, :] = -jnp.sin(angles) * factor
+
+    total = bs[k, lax.rem(q, 2), lax.div(q, 2)]
     for o in range(1, 16):
         scatter_bins(o).wait_recv()
         total = total + br[o]
@@ -312,7 +345,8 @@
             scatter_src(t, o).wait_send()
             gather_src(t, o).wait_send()
 
-    core_bins.wait_send()
+    for g in range(2):
+        core_bins(g).wait_send()
 
     @pl.loop(1, 16)
     def _(o):
@@ -346,20 +380,20 @@
             pltpu.VMEM((T, 32, NS, C), BF),
             pltpu.VMEM((NBIN, C), jnp.int32),
             pltpu.VMEM((8, NBIN, 8 * C), BF),
-            pltpu.VMEM((NBIN, C), F32),
+            pltpu.VMEM((NBIN, C), BF),
             pltpu.VMEM((NS * 2 * FD, C), F32),
             pltpu.VMEM((4, 2 * C, 8 * C), BF),
             pltpu.VMEM((2 * FD, NLAG), F32),
-            pltpu.VMEM((2, 16, 40, C), F32),
-            pltpu.VMEM((16, 40, C), F32),
-            pltpu.VMEM((16, 40, C), F32),
+            pltpu.VMEM((2, 2, 8, 33, C), F32),
+            pltpu.VMEM((2, 8, 33, C), F32),
+            pltpu.VMEM((16, 33, C), F32),
             pltpu.VMEM((4, 8, NLAG), F32),
             pltpu.VMEM((4, 8, NLAG), F32),
             pltpu.VMEM((8, NLAG), F32),
             pltpu.VMEM((4, 8, NLAG), F32),
             pltpu.VMEM((4, 8, NLAG), F32),
             dma, dma((T,)), dma((T,)), dma((T, 16)), dma((T, 16)), dma((T, 16)), dma((T, 16)), dma((T, 16)), dma((T, 16)),
-            dma, dma, dma((16,)), dma((16,)), dma((4,)), dma((4,)), dma((4,)), dma((4,)), dma((4,)), dma((4,)),
+            dma((2,)), dma((2,)), dma((16,)), dma((16,)), dma((4,)), dma((4,)), dma((4,)), dma((4,)), dma((4,)), dma((4,)),
         ],
         compiler_params=pltpu.CompilerParams(
             collective_id=0, has_side_effects=True, vmem_limit_bytes=56 * 1024 * 1024),

time: 70 us -> 67.6 us (0.966)
  the two profiles are of different devices: /device:TPU:4 before, /device:TPU:32 now
where the time goes in v3:
time: 67.6 us; the launch traced here: 67.4 us
  Pallas kernels  65.9 us (97%)
  other arithmetic  1.4 us (2%)
    pallas_call x1, Pallas kernels, body(): pl.pallas_call(kernel, out_shape=[jax.ShapeDtypeStruct((4, 8, NLAG), F32)...  65.9 us
    div x1, other arithmetic, body(): return sums.reshape(32, NLAG) / norm  1.4 us

profile of v3, /device:TPU:32, one launch (start us, length us, event | category | flops | bytes accessed | tf_op | source)
XLA Modules:
  0.0 67.4 jit_solution(1814729631687218815)
XLA Ops:
  0.0 65.9 %shard_map.46 = (f32[4,8,256]{2,1,0:T(8,128)}, f32[32,256]{1,0:T(8,128)}) custom-call(s32[2,32]{1,0:T(2,128)} %src_ref.1, bf16[2,30,64,128]{3,2,1,0:T(8,128)(2,1)} %spec_hbm.1, s32[64,128]{1,0:T(8,128)} %bitcast.4, s32[8,128]{1,0:T(8,128)} %bitcast.5), custom_call_target="tpu_custom_call" | custom-call | tf_op jit(solution)/shard_map/pallas_call | solution.py:366
  66.0 1.4 %bitcast_divide_fusion = f32[32,256]{1,0:T(8,128)} fusion(f32[32,256]{1,0:T(8,128)} %get-tuple-element.8, f32[4,8,256]{2,1,0:T(8,128)} %get-tuple-element.7), kind=kLoop, calls=%fused_computation | loop fusion | flops 8192 | bytes 98304 | tf_op jit(solution)/shard_map/div | solution.py:401

commit v4 on v3

--- a/solution.py
+++ b/solution.py
@@ -290,15 +290,22 @@
     shift = lax.broadcasted_iota(jnp.int32, (FD, NLAG), 1) - NLAG // 2
     angles = ((tone * shift) & (2 * F - 1)).astype(F32) * (math.pi / F)
     factor = 1.0 / math.sqrt(W * F)
-    basis[:FD, :] = jnp.cos(angles) * factor
-    basis[FD:, :] = -jnp.sin(angles) * factor
+    table = jnp.concatenate([jnp.cos(angles), -jnp.sin(angles)], axis=0) * factor
+    high = table.astype(BF)
+    basis[:, :NLAG] = high
+    basis[:, NLAG:] = (table - high.astype(F32)).astype(BF)
 
     total = bs[k, lax.rem(q, 2), lax.div(q, 2)]
     for o in range(1, 16):
         scatter_bins(o).wait_recv()
         total = total + br[o]
 
-    traces = jnp.dot(total[:32], basis[...], precision=lax.Precision.HIGHEST, preferred_element_type=F32)
+    stacks = total[:32]
+    stacks_hi = stacks.astype(BF)
+    stacks_lo = (stacks - stacks_hi.astype(F32)).astype(BF)
+    both = jnp.concatenate([stacks_hi, stacks_lo], axis=0)
+    got = jnp.dot(both, basis[...], preferred_element_type=F32)
+    traces = got[:32, :NLAG] + (got[32:, :NLAG] + got[:32, NLAG:]) + got[32:, NLAG:]
     for part in range(4):
         lag[part] = traces[part * 8 : part * 8 + 8]
 
@@ -383,7 +390,7 @@
             pltpu.VMEM((NBIN, C), BF),
             pltpu.VMEM((NS * 2 * FD, C), F32),
             pltpu.VMEM((4, 2 * C, 8 * C), BF),
-            pltpu.VMEM((2 * FD, NLAG), F32),
+            pltpu.VMEM((2 * FD, 2 * NLAG), BF),
             pltpu.VMEM((2, 2, 8, 33, C), F32),
             pltpu.VMEM((2, 8, 33, C), F32),
             pltpu.VMEM((16, 33, C), F32),

time: 67.6 us -> 67.6 us (level)
  no operation moved by 1% of the time
where the time goes in v4:
time: 67.6 us; the launch traced here: 67.3 us
  Pallas kernels  65.9 us (97%)
  other arithmetic  1.4 us (2%)
    pallas_call x1, Pallas kernels, body(): pl.pallas_call(kernel, out_shape=[jax.ShapeDtypeStruct((4, 8, NLAG), F32)...  65.9 us
    div x1, other arithmetic, body(): return sums.reshape(32, NLAG) / norm  1.4 us

profile of v4, /device:TPU:32, one launch (start us, length us, event | category | flops | bytes accessed | tf_op | source)
XLA Modules:
  0.0 67.3 jit_solution(16385876638992109786)
XLA Ops:
  0.0 65.9 %shard_map.46 = (f32[4,8,256]{2,1,0:T(8,128)}, f32[32,256]{1,0:T(8,128)}) custom-call(s32[2,32]{1,0:T(2,128)} %src_ref.1, bf16[2,30,64,128]{3,2,1,0:T(8,128)(2,1)} %spec_hbm.1, s32[64,128]{1,0:T(8,128)} %bitcast.4, s32[8,128]{1,0:T(8,128)} %bitcast.5), custom_call_target="tpu_custom_call" | custom-call | tf_op jit(solution)/shard_map/pallas_call | solution.py:373
  65.9 1.4 %bitcast_divide_fusion = f32[32,256]{1,0:T(8,128)} fusion(f32[32,256]{1,0:T(8,128)} %get-tuple-element.8, f32[4,8,256]{2,1,0:T(8,128)} %get-tuple-element.7), kind=kLoop, calls=%fused_computation | loop fusion | flops 8192 | bytes 98304 | tf_op jit(solution)/shard_map/div | solution.py:408
